TPU v7x, 128 devices: a whole 4x4x4 slice. The times are simulated.
128 devices in a mesh: lon: 32 (over y, z, x_lo), ch: 4 (over x_hi, core).
Axes of the slice: x: 4 (x_hi: 2, x_lo: 2; x = x_hi * 2 + x_lo), y: 4, z: 4, core: 2. Of those that a mesh axis runs over, the one named last changes fastest.
Arguments:
- features: bfloat16 [1024, 1, 576, 128], P('ch', None, 'lon'), may hold values from -6 to 6
- cotangent: bfloat16 [3, 256, 1, 576, 128], P(None, 'ch', None, 'lon'), may hold values from -6 to 6
- weights: bfloat16 [3, 3, 3, 256, 1024], P(None, None, None, 'ch'), may hold values from -0.0625 to 0.0625
Outputs:
- input_grad: bfloat16 [1024, 1, 576, 128], P('ch', None, 'lon')
- kernel_grad: float32 [3, 3, 3, 256, 1024], P(None, None, None, 'ch')
All inputs are finite; a program needn't handle non-finite values.
Results may differ from a plain program's by a relative error of at most 0.001.
Values may be sent and summed in bfloat16 or wider, within the bound.
A program may use at most 256 MiB of HBM per device.

v0:
```python
import jax
import jax.numpy as jnp
from jax import lax
from jax.sharding import PartitionSpec as P

DILATIONS = (6, 12, 18)
RIM = 18


def with_halo(cells, sides, width):
    for axis, dim in sides:
        count = lax.axis_size(axis)
        head = lax.slice_in_dim(cells, 0, width, axis=dim)
        tail = lax.slice_in_dim(cells, cells.shape[dim] - width, cells.shape[dim], axis=dim)
        cells = jnp.concatenate(
            [
                lax.ppermute(tail, axis, [(i, (i + 1) % count) for i in range(count)]),
                cells,
                lax.ppermute(head, axis, [((i + 1) % count, i) for i in range(count)]),
            ],
            axis=dim,
        )
    return cells


def filter_terms(cotangent, widened):
    lon_cols = cotangent.shape[3]
    lat_rows = cotangent.shape[4]
    padded = jnp.pad(widened, ((0, 0), (0, 0), (0, 0), (RIM, RIM)))
    results = []
    for branch in range(3):
        dilation = DILATIONS[branch]
        for lat_tap in range(3):
            for lon_tap in range(3):
                lon_start = RIM + dilation * (lon_tap - 1)
                lat_start = RIM + dilation * (lat_tap - 1)
                window = padded[
                    :, :, lon_start : lon_start + lon_cols, lat_start : lat_start + lat_rows
                ]
                results.append(
                    lax.dot_general(
                        cotangent[branch],
                        window,
                        (((1, 2, 3), (1, 2, 3)), ((), ())),
                        preferred_element_type=jnp.float32,
                    )
                )
    stacked = jnp.stack(results)
    return stacked.reshape(3, 3, 3, stacked.shape[1], stacked.shape[2])


def branch_taps(grad_ext, offset, dilation, lon_cols, lat_rows):
    grad_pad = jnp.pad(grad_ext, ((0, 0), (0, 0), (0, 0), (dilation, dilation)))
    slices = []
    for lat_tap in range(3):
        for lon_tap in range(3):
            lon_start = offset - dilation * (lon_tap - 1)
            lat_start = dilation - dilation * (lat_tap - 1)
            slices.append(
                grad_pad[:, :, lon_start : lon_start + lon_cols, lat_start : lat_start + lat_rows]
            )
    return jnp.concatenate(slices, axis=0)


def local(features, cotangent, weights):
    in_rows = features.shape[0]
    in_total = weights.shape[4]
    samples = features.shape[1]
    lon_cols = features.shape[2]
    lat_rows = features.shape[3]
    cells_here = samples * lon_cols * lat_rows
    whole = lax.all_gather(features, "ch", axis=0, tiled=True)
    widened = with_halo(whole, (("lon", 2),), RIM)
    partial_kernel = filter_terms(cotangent, widened)
    cells_all = cells_here * lax.axis_size("lon")
    kernel_grad = lax.psum(partial_kernel, "lon") / jnp.sqrt(jnp.float32(cells_all))
    grad_wide = with_halo(cotangent, (("lon", 3),), RIM)
    extended = [grad_wide[0], grad_wide[1], grad_wide[2]]
    offsets = [RIM, RIM, RIM]
    grad_stack = jnp.concatenate(
        [branch_taps(extended[k], offsets[k], DILATIONS[k], lon_cols, lat_rows) for k in range(3)],
        axis=0,
    ).reshape(-1, cells_here)
    kernel_matrix = weights.reshape(-1, in_total)
    product = lax.dot_general(
        kernel_matrix, grad_stack, (((0,), (0,)), ((), ())), preferred_element_type=jnp.float32
    )
    input_grad = lax.psum_scatter(
        product.reshape(lax.axis_size("ch") * in_rows, samples, lon_cols, lat_rows),
        "ch",
        scatter_dimension=0,
        tiled=True,
    ).astype(jnp.bfloat16)
    return (input_grad, kernel_grad)


def solution(mesh):
    return jax.shard_map(
        local,
        mesh=mesh,
        in_specs=(
            P("ch", None, "lon", None),
            P(None, "ch", None, "lon", None),
            P(None, None, None, "ch", None),
        ),
        out_specs=(P("ch", None, "lon", None), P(None, None, None, "ch", None)),
        check_vma=False,
    )
```

profile of v0, /device:TPU:1, one launch (start us, length us, event | category | flops | bytes accessed | tf_op | source)
XLA Modules:
  0.0 891.6 jit_solution(3159787470432086120)
XLA Ops:
  8.0 46.9 %all-gather.2.cloned.1.call-done = bf16[1024,1,18,128]{3,0,2,1:T(8,128)(2,1)} async-done(((bf16[256,1,18,128]{3,0,2,1:T(8,128)(2,1)}), bf16[1024,1,18,128]{3,0,2,1:T(8,128)(2,1)}) %all-gather.2.cloned.1.call-update) | async-done | bytes 4718608 | tf_op jit(solution)/shard_map/all_gather | solution.py:72
  59.7 5.7 collective-permute-start.1
  65.4 217.4 %collective-permute-done = bf16[3,64,1,18,128]{4,1,3,2,0:T(8,128)(2,1)S(1)} collective-permute-done((bf16[3,64,1,18,128]{4,1,3,2,0:T(8,128)(2,1)}, bf16[3,64,1,18,128]{4,1,3,2,0:T(8,128)(2,1)S(1)}, u32[]{:S(2)}, u32[]{:S(2)}) %collective-permute-start) | collective-permute-done | bytes 884768 | tf_op jit(solution)/shard_map/ppermute | solution.py:17
  283.9 21.6 %fusion.5 = bf16[1024,1,54,164]{3,0,2,1:T(8,128)(2,1)} fusion(bf16[1024,1,18,128]{3,0,2,1:T(8,128)(2,1)} %collective-permute-done.3, bf16[1024,1,18,128]{3,0,2,1:T(8,128)(2,1)} %all-gather.2.cloned.1.call-done, bf16[1024,1,18,128]{3,0,2,1:T(8,128)(2,1)} %collective-permute-done.2), kind=kLoop, calls=%fused_computation.7 | loop fusion | flops 108822528 | bytes 32292864 | tf_op jit(solution)/shard_map/concatenate | solution.py:15
  305.6 5.9 fusion.69
  311.5 6.0 fusion.71
  317.4 5.9 fusion.73
  328.2 5.8 constant_dynamic-update-slice_fusion.6
  345.1 5.8 fusion.79
  350.9 6.0 fusion.81
  357.0 5.8 fusion.83
  362.8 5.8 fusion.85
  368.6 6.0 fusion.87
  374.6 5.9 fusion.89
  385.1 6.2 fusion.95
  391.3 5.8 fusion.97
  397.2 5.8 fusion.99
  424.7 6.0 fusion.107
  468.2 11.9 %copy.6 = bf16[1728,1,18,128]{0,3,2,1:T(8,128)(2,1)} copy(bf16[1728,1,18,128]{3,0,2,1:T(8,128)(2,1)} %fusion.129) | data formatting | bytes 15925248 | tf_op jit(solution)/shard_map/concatenate | solution.py:80
  480.1 13.2 %fusion.184 = f32[2304,1024]{1,0:T(8,128)} fusion(bf16[1728,2304]{0,1:T(8,128)(2,1)} %bitcast.465, bf16[1728,1024]{1,0:T(8,128)(2,1)S(1)} %bitcast.459), kind=kOutput, calls=%fused_computation.226 | convolution fusion | flops 8153726976 | bytes 20938752 | tf_op jit(solution)/shard_map/dot_general | solution.py:85
  493.3 9.7 %copy.7 = f32[1024,1,18,128]{3,0,2,1:T(8,128)} copy(f32[1024,1,18,128]{0,3,2,1:T(8,128)} %bitcast.464) | data formatting | bytes 18874368 | tf_op jit(solution)/shard_map/reshape | solution.py:89
  503.0 276.2 %all-reduce.6.cloned.1.call-done = f32[3,3,3,64,1024]{4,3,2,1,0:T(8,128)} async-done(((f32[3,3,3,64,1024]{4,3,2,1,0:T(8,128)}), f32[3,3,3,64,1024]{4,3,2,1,0:T(8,128)}) %all-reduce.6.cloned.1.call-update) | async-done | bytes 7077904 | tf_op jit(solution)/shard_map/psum | solution.py:76
  779.2 7.6 broadcast_multiply_fusion
  786.8 95.1 %reduce-scatter.2.cloned.1.call-done = f32[256,1,18,128]{3,0,2,1:T(8,128)} async-done(((f32[1024,1,18,128]{3,0,2,1:T(8,128)}), f32[256,1,18,128]{3,0,2,1:T(8,128)}) %reduce-scatter.2.cloned.1.call-update) | async-done | bytes 2359312 | tf_op jit(solution)/shard_map/reduce_scatter | solution.py:88
  (95 shorter events, 89.3 us)
Async XLA Ops:
  7.2 472.9 %copy-start = (bf16[3,3,3,64,1024]{4,3,2,1,0:T(8,128)(2,1)S(1)}, bf16[3,3,3,64,1024]{4,3,2,1,0:T(8,128)(2,1)}, u32[]{:S(2)}) copy-start(bf16[3,3,3,64,1024]{4,3,2,1,0:T(8,128)(2,1)} %param.5) | copy-start | bytes 10616836
  7.2 47.6 %all-gather.2.cloned.1.call-start = ((), (), s32[]{:S(2)}) async-start(), calls=%async_computation.2 | async-start | bytes 5898240 | tf_op jit(solution)/shard_map/all_gather | solution.py:72
  7.9 771.2 %all-reduce.6.cloned.1.call-start = ((), (), s32[]{:S(2)}) async-start(), calls=%async_computation.3 | async-start | bytes 14155776 | tf_op jit(solution)/shard_map/psum | solution.py:76
  54.8 229.1 %collective-permute-start.3 = (bf16[1024,1,18,128]{3,0,2,1:T(8,128)(2,1)}, bf16[1024,1,18,128]{3,0,2,1:T(8,128)(2,1)}, u32[]{:S(2)}, u32[]{:S(2)}) collective-permute-start(bf16[1024,1,18,128]{3,0,2,1:T(8,128)(2,1)} %all-gather.2.cloned.1.call-done), channel_id=1, source_target_pairs={{4,0},{8,4},{12,8},{16,12},{20,16},{24,20},{28,24},{32,28},{36,32}... | collective-permute-start | bytes 14155784 | tf_op jit(solution)/shard_map/ppermute | solution.py:19
  59.7 224.2 %collective-permute-start.2 = (bf16[1024,1,18,128]{3,0,2,1:T(8,128)(2,1)}, bf16[1024,1,18,128]{3,0,2,1:T(8,128)(2,1)}, u32[]{:S(2)}, u32[]{:S(2)}) collective-permute-start(bf16[1024,1,18,128]{3,0,2,1:T(8,128)(2,1)} %all-gather.2.cloned.1.call-done), channel_id=1, source_target_pairs={{0,4},{4,8},{8,12},{12,16},{16,20},{20,24},{24,28},{28,32},{32,36}... | collective-permute-start | bytes 14155784 | tf_op jit(solution)/shard_map/ppermute | solution.py:17
  59.7 223.1 %collective-permute-start = (bf16[3,64,1,18,128]{4,1,3,2,0:T(8,128)(2,1)}, bf16[3,64,1,18,128]{4,1,3,2,0:T(8,128)(2,1)S(1)}, u32[]{:S(2)}, u32[]{:S(2)}) collective-permute-start(bf16[3,64,1,18,128]{4,1,3,2,0:T(8,128)(2,1)} %param.4), channel_id=1, source_target_pairs={{0,4},{4,8},{8,12},{12,16},{16,20},{20,24},{24,28},{28,32},{32,36}... | collective-permute-start | bytes 2654216 | tf_op jit(solution)/shard_map/ppermute | solution.py:17
  59.7 380.8 %collective-permute-start.1 = (bf16[3,64,1,18,128]{4,1,3,2,0:T(8,128)(2,1)}, bf16[3,64,1,18,128]{4,1,3,2,0:T(8,128)(2,1)}, u32[]{:S(2)}, u32[]{:S(2)}) collective-permute-start(bf16[3,64,1,18,128]{4,1,3,2,0:T(8,128)(2,1)} %param.4), channel_id=1, source_target_pairs={{4,0},{8,4},{12,8},{16,12},{20,16},{24,20},{28,24},{32,28},{36,32}... | collective-permute-start | bytes 2654216 | tf_op jit(solution)/shard_map/ppermute | solution.py:19
  305.5 5.9 copy-start.2
  311.4 16.7 %slice-start = ((s8[4718592]{0:T(1024)(128)(4,1)}), s8[4194304]{0:T(1024)(128)(4,1)S(1)}, s32[]{:S(2)}) async-start(s8[4718592]{0:T(1024)(128)(4,1)} %bitcast.460), calls=%async_computation.4 | async-start | bytes 8388608
  317.4 10.7 %slice-start.1 = ((s8[4718592]{0:T(1024)(128)(4,1)}), s8[524288]{0:T(1024)(128)(4,1)S(1)}, s32[]{:S(2)}) async-start(s8[4718592]{0:T(1024)(128)(4,1)} %bitcast.460), calls=%async_computation.5 | async-start | bytes 1048576
  333.9 5.1 copy-start.3
  368.6 11.9 %slice-start.9 = ((s8[9437184]{0:T(1024)(128)(4,1)}), s8[4194304]{0:T(1024)(128)(4,1)S(1)}, s32[]{:S(2)}) async-start(s8[9437184]{0:T(1024)(128)(4,1)} %bitcast.467), calls=%async_computation.13 | async-start | bytes 8388608
  368.6 11.9 %slice-start.10 = ((s8[9437184]{0:T(1024)(128)(4,1)}), s8[4194304]{0:T(1024)(128)(4,1)S(1)}, s32[]{:S(2)}) async-start(s8[9437184]{0:T(1024)(128)(4,1)} %bitcast.467), calls=%async_computation.14 | async-start | bytes 8388608
  374.6 5.9 slice-start.11
  403.0 27.7 %slice-start.2 = ((s8[28311552]{0:T(1024)(128)(4,1)}), s8[4194304]{0:T(1024)(128)(4,1)S(1)}, s32[]{:S(2)}) async-start(s8[28311552]{0:T(1024)(128)(4,1)} %bitcast.462), calls=%async_computation.6 | async-start | bytes 8388608
  403.0 27.7 %slice-start.3 = ((s8[28311552]{0:T(1024)(128)(4,1)}), s8[4194304]{0:T(1024)(128)(4,1)S(1)}, s32[]{:S(2)}) async-start(s8[28311552]{0:T(1024)(128)(4,1)} %bitcast.462), calls=%async_computation.7 | async-start | bytes 8388608
  407.0 23.6 %slice-start.4 = ((s8[28311552]{0:T(1024)(128)(4,1)}), s8[4194304]{0:T(1024)(128)(4,1)S(1)}, s32[]{:S(2)}) async-start(s8[28311552]{0:T(1024)(128)(4,1)} %bitcast.462), calls=%async_computation.8 | async-start | bytes 8388608
  411.0 19.6 %slice-start.5 = ((s8[28311552]{0:T(1024)(128)(4,1)}), s8[4194304]{0:T(1024)(128)(4,1)S(1)}, s32[]{:S(2)}) async-start(s8[28311552]{0:T(1024)(128)(4,1)} %bitcast.462), calls=%async_computation.9 | async-start | bytes 8388608
  415.1 15.6 %slice-start.6 = ((s8[28311552]{0:T(1024)(128)(4,1)}), s8[4194304]{0:T(1024)(128)(4,1)S(1)}, s32[]{:S(2)}) async-start(s8[28311552]{0:T(1024)(128)(4,1)} %bitcast.462), calls=%async_computation.10 | async-start | bytes 8388608
  420.6 10.1 %slice-start.7 = ((s8[28311552]{0:T(1024)(128)(4,1)}), s8[4194304]{0:T(1024)(128)(4,1)S(1)}, s32[]{:S(2)}) async-start(s8[28311552]{0:T(1024)(128)(4,1)} %bitcast.462), calls=%async_computation.11 | async-start | bytes 8388608
  424.7 6.0 slice-start.8
  435.2 3.0 copy-start.1
  438.2 443.8 %reduce-scatter.2.cloned.1.call-start = ((), (), s32[]{:S(2)}) async-start(), calls=%async_computation.1 | async-start | bytes 11796480 | tf_op jit(solution)/shard_map/reduce_scatter | solution.py:88
Sparse Core Ops, SparseCore 0:
  9.7 45.0 all-gather.1
  438.3 340.8 all-reduce.5
  781.9 100.0 reduce-scatter.1
where the time goes:
time: 896 us; the launch traced here: 892 us
  waiting for transfers between devices  636 us (71%)
  matrix products  128 us (14%)
  local copies, waits for them, and re-layouts  70.3 us (8%)
  other arithmetic  32.2 us (4%)
  between operations  14.2 us (2%)
  starting transfers between devices  10.7 us (1%)
    psum x1, waiting for transfers between devices, local(): lax.psum(partial_kernel, 'lon') / jnp.sqrt(jnp.float32(cells_all))  276 us
    ppermute x2, waiting for transfers between devices, with_halo(): lax.ppermute(tail, axis, [(i, (i + 1) % count) for i in range(count)])  217 us
    dot_general x27, matrix products, filter_terms(): lax.dot_general(cotangent[branch], window, (((1, 2, 3), (1, 2, 3)), ((),...  115 us
    reduce_scatter x1, waiting for transfers between devices, local(): lax.psum_scatter(product.reshape(lax.axis_size('ch') * in_rows, samples,...  95.1 us
    all_gather x1, waiting for transfers between devices, local(): whole = lax.all_gather(features, 'ch', axis=0, tiled=True)  46.9 us
    unnamed x62, local copies, waits for them, and re-layouts  40.3 us
    concatenate x1, other arithmetic, with_halo(): jnp.concatenate([lax.ppermute(tail, axis, [(i, (i + 1) % count) for i in...  21.6 us
  transfers between devices with their start and end apart: 7, of which 4 were waited for; matrix products, arithmetic and copies ran while one was open for 25% of the time, Pallas kernels for 0%

commit v1 on v0

--- a/solution.py
+++ b/solution.py
@@ -69,7 +69,9 @@
     lon_cols = features.shape[2]
     lat_rows = features.shape[3]
     cells_here = samples * lon_cols * lat_rows
-    whole = lax.all_gather(features, "ch", axis=0, tiled=True)
+    whole = jnp.concatenate(
+        lax.all_to_all(jnp.stack([features] * lax.axis_size("ch")), "ch", 0, 0), axis=0
+    )
     widened = with_halo(whole, (("lon", 2),), RIM)
     partial_kernel = filter_terms(cotangent, widened)
     cells_all = cells_here * lax.axis_size("lon")

time: 896 us -> 864 us (0.964)
  the two profiles are of different devices: /device:TPU:1 before, /device:TPU:0 now
where the time goes in v1:
time: 864 us; the launch traced here: 859 us
  waiting for transfers between devices  557 us (64%)
  matrix products  121 us (14%)
  blocking collectives  59.5 us (7%)
  local copies, waits for them, and re-layouts  59.4 us (7%)
  other arithmetic  32.2 us (4%)
  between operations  15.8 us (2%)
  starting transfers between devices  13.7 us (2%)
    psum x1, waiting for transfers between devices, local(): lax.psum(partial_kernel, 'lon') / jnp.sqrt(jnp.float32(cells_all))  342 us
    ppermute x2, waiting for transfers between devices, with_halo(): lax.ppermute(tail, axis, [(i, (i + 1) % count) for i in range(count)])  214 us
    dot_general x27, matrix products, filter_terms(): lax.dot_general(cotangent[branch], window, (((1, 2, 3), (1, 2, 3)), ((),...  108 us
    all_to_all x1, blocking collectives, local(): lax.all_to_all(jnp.stack([features] * lax.axis_size('ch')), 'ch', 0, 0)  59.5 us
    unnamed x56, local copies, waits for them, and re-layouts  29.3 us
    concatenate x1, other arithmetic, with_halo(): jnp.concatenate([lax.ppermute(tail, axis, [(i, (i + 1) % count) for i in...  21.7 us
  transfers between devices with their start and end apart: 6, of which 2 were waited for; matrix products, arithmetic and copies ran while one was open for 24% of the time, Pallas kernels for 0%

profile of v1, /device:TPU:0, one launch (start us, length us, event | category | flops | bytes accessed | tf_op | source)
XLA Modules:
  0.0 858.8 jit_solution(1945396272823157130)
XLA Ops:
  10.7 59.5 %all_to_all.5 = bf16[4,256,1,18,128]{4,1,3,2,0:T(8,128)(2,1)S(1)} all-to-all(bf16[4,256,1,18,128]{4,1,3,2,0:T(8,128)(2,1)S(1)} %stack.91), channel_id=1, replica_groups=mesh['lon'=32,'ch'=4] {'ch'}, dimensions={0} | all-to-all | bytes 9437184 | tf_op jit(solution)/shard_map/all_to_all | solution.py:73
  73.0 6.5 collective-permute-start.3
  79.5 6.2 collective-permute-start.1
  85.8 214.4 %collective-permute-done = bf16[3,64,1,18,128]{4,1,3,2,0:T(8,128)(2,1)S(1)} collective-permute-done((bf16[3,64,1,18,128]{4,1,3,2,0:T(8,128)(2,1)}, bf16[3,64,1,18,128]{4,1,3,2,0:T(8,128)(2,1)S(1)}, u32[]{:S(2)}, u32[]{:S(2)}) %collective-permute-start) | collective-permute-done | bytes 884768 | tf_op jit(solution)/shard_map/ppermute | solution.py:17
  303.4 21.7 %fusion.5 = bf16[1024,1,54,164]{3,0,2,1:T(8,128)(2,1)} fusion(bf16[1024,1,18,128]{3,0,2,1:T(8,128)(2,1)} %collective-permute-done.3, bf16[1024,1,18,128]{3,0,2,1:T(8,128)(2,1)} %bitcast.449, bf16[1024,1,18,128]{3,0,2,1:T(8,128)(2,1)} %copy-done.2), kind=kLoop, calls=%fused_computation.7 | loop fusion | flops 108822528 | bytes 32292864 | tf_op jit(solution)/shard_map/concatenate | solution.py:15
  325.1 6.7 fusion.57
  331.7 6.7 fusion.59
  338.4 6.7 fusion.61
  355.7 3.8 fusion.63
  363.4 4.0 fusion.67
  367.4 3.8 fusion.69
  371.2 3.8 fusion.71
  375.0 3.8 fusion.73
  385.3 4.1 fusion.116
  393.2 4.2 fusion.77
  397.4 3.8 fusion.79
  417.3 4.7 fusion.53
  425.8 3.8 fusion.89
  429.6 3.8 fusion.91
  463.6 11.7 %copy.8 = bf16[1728,1,18,128]{0,3,2,1:T(8,128)(2,1)} copy(bf16[1728,1,18,128]{3,0,2,1:T(8,128)(2,1)} %fusion.136) | data formatting | bytes 15925248 | tf_op jit(solution)/shard_map/concatenate | solution.py:82
  475.3 13.2 %fusion.195 = f32[2304,1024]{1,0:T(8,128)} fusion(bf16[1728,2304]{0,1:T(8,128)(2,1)} %bitcast.464, bf16[1728,1024]{1,0:T(8,128)(2,1)S(1)} %bitcast.446), kind=kOutput, calls=%fused_computation.230 | convolution fusion | flops 8153726976 | bytes 20938752 | tf_op jit(solution)/shard_map/dot_general | solution.py:87
  488.6 9.6 %copy.9 = f32[1024,1,18,128]{3,0,2,1:T(8,128)} copy(f32[1024,1,18,128]{0,3,2,1:T(8,128)} %bitcast.463) | data formatting | bytes 18874368 | tf_op jit(solution)/shard_map/reshape | solution.py:91
  498.3 342.4 %all-reduce.6.cloned.1.call-done = f32[3,3,3,64,1024]{4,3,2,1,0:T(8,128)} async-done(((f32[3,3,3,64,1024]{4,3,2,1,0:T(8,128)}), f32[3,3,3,64,1024]{4,3,2,1,0:T(8,128)}) %all-reduce.6.cloned.1.call-update) | async-done | bytes 7077904 | tf_op jit(solution)/shard_map/psum | solution.py:78
  840.6 7.6 broadcast_multiply_fusion
  (88 shorter events, 86.3 us)
Async XLA Ops:
  8.0 467.3 %copy-start = (bf16[3,3,3,64,1024]{4,3,2,1,0:T(8,128)(2,1)S(1)}, bf16[3,3,3,64,1024]{4,3,2,1,0:T(8,128)(2,1)}, u32[]{:S(2)}) copy-start(bf16[3,3,3,64,1024]{4,3,2,1,0:T(8,128)(2,1)} %param.5) | copy-start | bytes 10616836
  8.0 832.6 %all-reduce.6.cloned.1.call-start = ((), (), s32[]{:S(2)}) async-start(), calls=%async_computation.3 | async-start | bytes 14155776 | tf_op jit(solution)/shard_map/psum | solution.py:78
  70.8 2.2 copy-start.1
  70.8 230.4 %collective-permute-start.2 = (bf16[1024,1,18,128]{3,0,2,1:T(8,128)(2,1)S(1)}, bf16[1024,1,18,128]{3,0,2,1:T(8,128)(2,1)S(1)}, u32[]{:S(2)}, u32[]{:S(2)}) collective-permute-start(bf16[1024,1,18,128]{3,0,2,1:T(8,128)(2,1)S(1)} %bitcast.447), channel_id=1, source_target_pairs={{0,4},{4,8},{8,12},{12,16},{16,20},{20,24},{24,28},{28,32},{32,36}... | collective-permute-start | bytes 14155784 | tf_op jit(solution)/shard_map/ppermute | solution.py:17
  73.0 230.4 %collective-permute-start.3 = (bf16[1024,1,18,128]{3,0,2,1:T(8,128)(2,1)S(1)}, bf16[1024,1,18,128]{3,0,2,1:T(8,128)(2,1)}, u32[]{:S(2)}, u32[]{:S(2)}) collective-permute-start(bf16[1024,1,18,128]{3,0,2,1:T(8,128)(2,1)S(1)} %bitcast.448), channel_id=1, source_target_pairs={{4,0},{8,4},{12,8},{16,12},{20,16},{24,20},{28,24},{32,28},{36,32}... | collective-permute-start | bytes 14155784 | tf_op jit(solution)/shard_map/ppermute | solution.py:19
  79.5 220.6 %collective-permute-start = (bf16[3,64,1,18,128]{4,1,3,2,0:T(8,128)(2,1)}, bf16[3,64,1,18,128]{4,1,3,2,0:T(8,128)(2,1)S(1)}, u32[]{:S(2)}, u32[]{:S(2)}) collective-permute-start(bf16[3,64,1,18,128]{4,1,3,2,0:T(8,128)(2,1)} %param.4), channel_id=1, source_target_pairs={{0,4},{4,8},{8,12},{12,16},{16,20},{20,24},{24,28},{28,32},{32,36}... | collective-permute-start | bytes 2654216 | tf_op jit(solution)/shard_map/ppermute | solution.py:17
  79.5 356.4 %collective-permute-start.1 = (bf16[3,64,1,18,128]{4,1,3,2,0:T(8,128)(2,1)}, bf16[3,64,1,18,128]{4,1,3,2,0:T(8,128)(2,1)}, u32[]{:S(2)}, u32[]{:S(2)}) collective-permute-start(bf16[3,64,1,18,128]{4,1,3,2,0:T(8,128)(2,1)} %param.4), channel_id=1, source_target_pairs={{4,0},{8,4},{12,8},{16,12},{20,16},{24,20},{28,24},{32,28},{36,32}... | collective-permute-start | bytes 2654216 | tf_op jit(solution)/shard_map/ppermute | solution.py:19
  301.2 2.1 copy-start.2
  325.1 20.0 %slice-start.9 = ((s8[4718592]{0:T(1024)(128)(4,1)}), s8[4194304]{0:T(1024)(128)(4,1)S(1)}, s32[]{:S(2)}) async-start(s8[4718592]{0:T(1024)(128)(4,1)} %bitcast.461), calls=%async_computation.13 | async-start | bytes 8388608
  331.7 13.3 %slice-start = ((s8[4718592]{0:T(1024)(128)(4,1)}), s8[4194304]{0:T(1024)(128)(4,1)S(1)}, s32[]{:S(2)}) async-start(s8[4718592]{0:T(1024)(128)(4,1)} %bitcast.450), calls=%async_computation.4 | async-start | bytes 8388608
  331.7 13.3 %slice-start.10 = ((s8[4718592]{0:T(1024)(128)(4,1)}), s8[524288]{0:T(1024)(128)(4,1)S(1)}, s32[]{:S(2)}) async-start(s8[4718592]{0:T(1024)(128)(4,1)} %bitcast.461), calls=%async_computation.14 | async-start | bytes 1048576
  338.4 6.7 slice-start.1
  338.4 17.3 %slice-start.2 = ((s8[28311552]{0:T(1024)(128)(4,1)}), s8[4194304]{0:T(1024)(128)(4,1)S(1)}, s32[]{:S(2)}) async-start(s8[28311552]{0:T(1024)(128)(4,1)} %bitcast.459), calls=%async_computation.6 | async-start | bytes 8388608
  338.4 17.3 %slice-start.3 = ((s8[28311552]{0:T(1024)(128)(4,1)}), s8[4194304]{0:T(1024)(128)(4,1)S(1)}, s32[]{:S(2)}) async-start(s8[28311552]{0:T(1024)(128)(4,1)} %bitcast.459), calls=%async_computation.7 | async-start | bytes 8388608
  345.1 10.6 %slice-start.4 = ((s8[28311552]{0:T(1024)(128)(4,1)}), s8[4194304]{0:T(1024)(128)(4,1)S(1)}, s32[]{:S(2)}) async-start(s8[28311552]{0:T(1024)(128)(4,1)} %bitcast.459), calls=%async_computation.8 | async-start | bytes 8388608
  345.1 10.6 %slice-start.5 = ((s8[28311552]{0:T(1024)(128)(4,1)}), s8[4194304]{0:T(1024)(128)(4,1)S(1)}, s32[]{:S(2)}) async-start(s8[28311552]{0:T(1024)(128)(4,1)} %bitcast.459), calls=%async_computation.9 | async-start | bytes 8388608
  348.5 7.2 slice-start.6
  351.8 3.9 slice-start.7
  351.8 3.9 slice-start.8
  433.4 414.8 %reduce-scatter.2.cloned.1.call-start = ((), (), s32[]{:S(2)}) async-start(), calls=%async_computation.2 | async-start | bytes 11796480 | tf_op jit(solution)/shard_map/reduce_scatter | solution.py:90
Sparse Core Ops, SparseCore 0:
  433.6 407.0 all-reduce.5
Sparse Core Ops, SparseCore 1:
  498.3 88.6 reduce-scatter.1
